TPU v7x, 128 devices: a whole 4x4x4 slice. The times are simulated.
128 devices in a mesh: src: 8 (over x, core), dst: 16 (over z, y).
Axes of the slice: x: 4, y: 4, z: 4, core: 2. Of those that a mesh axis runs over, the one named last changes fastest.
Arguments:
- edge_state: bfloat16 [262144, 512], P(('src', 'dst')), may hold values from -6 to 6
- directions: float32 [3, 262144], P(None, ('src', 'dst')), as said below
- src_atom: int32 [262144], P(('src', 'dst')), may hold values from 0 to 511
- dst_atom: int32 [262144], P(('src', 'dst')), may hold values from 0 to 255
- rev_pos: int32 [262144], P(('src', 'dst')), may hold values from 0 to 15, as said below
- counts: int32 [128, 128], P(('src', 'dst')), may hold values from 0 to 16, as said below
- triplets: int32 [2048, 4], P(('src', 'dst')), may hold values from 0 to 127
- down_w: bfloat16 [2, 512, 64], replicated, may hold values from -0.25 to 0.25
- trip_w: bfloat16 [2, 256, 512], replicated, may hold values from -0.75 to 0.75
- edge_w: bfloat16 [2, 6, 512, 512], replicated, may hold values from -0.25 to 0.25
Outputs:
- new_state: bfloat16 [262144, 512], P(('src', 'dst'))
Inputs may be any that keep to these rules, and one draw needn't show every extreme that they name: `counts`: Symmetric, zero on the diagonal, and equal to 16 for some pair in every draw. Within each bucket b of device f, rev_pos maps the live positions one to one onto live positions of bucket f of device b, and the map for (b, f) is the inverse of that for (f, b); dead positions map to themselves. `directions`: unit vectors.
All inputs are finite; a program needn't handle non-finite values.
Results may differ from a plain program's by a relative error of at most 0.017.
Values may be sent and summed in bfloat16 or wider, within the bound.
A program may use at most 128 MiB of HBM per device.

v0:
```python
import jax
import jax.numpy as jnp
from jax import lax
from jax.experimental import pallas as pl
from jax.experimental.pallas import tpu as pltpu
from jax.sharding import PartitionSpec as P

BLK = 128
PAIRS = 4
NBLK = 2
NSPH = 4
TRIP = 64
DEGREE = 64
N_SRC = 8
N_DST = 16
DEVS = N_SRC * N_DST
CAP = 16
WIDTH = 512
ROWS = DEVS * CAP
CHUNK = N_DST * CAP
NBLOCK = ROWS // BLK
BPC = CHUNK // BLK
ATOM_ROWS = 256
PIECE = ATOM_ROWS // N_SRC
MESH = pl.DeviceIdType.MESH
F32 = jnp.float32
BF16 = jnp.bfloat16


def silu(value):
    half = 0.5 * value
    return half + half * jnp.tanh(half)


def dot(a, b):
    return jnp.dot(a, b, preferred_element_type=F32)


def loop(count, step):
    def body(i, carry):
        step(i)
        return carry

    lax.fori_loop(0, count, body, 0)


def kernel(
    tri,
    col,
    dirs_in,
    state_in,
    onehot_in,
    mirror_in,
    pick_in,
    down_in,
    trip_in,
    edge_in,
    out,
    state,
    base,
    msg,
    arr,
    refined,
    tiles,
    pool,
    dirs,
    onehot,
    mirror,
    pick,
    down,
    trip,
    edge,
    total,
    part,
    gathered,
    atoms,
    region,
    load_sem,
    out_sem,
    dirs_send,
    dirs_recv,
    pool_send,
    pool_recv,
    side_send,
    side_recv,
    msg_send,
    msg_recv,
    part_send,
    part_recv,
    atom_send,
    atom_recv,
):
    s = lax.axis_index("src")
    d = lax.axis_index("dst")
    me = s * N_DST + d
    x = s // 2
    core = s % 2
    twin = x * 2 + (1 - core)

    def remote(src, dst, send, recv, ts, td):
        return pltpu.make_async_remote_copy(
            src_ref=src,
            dst_ref=dst,
            send_sem=send,
            recv_sem=recv,
            device_id=(ts, td),
            device_id_type=MESH,
        )

    def drain(ref, sem):
        pltpu.make_async_copy(ref, ref, sem).wait()

    barrier = pltpu.get_barrier_semaphore()

    def greet(i):
        t = (me + 1 + i) % DEVS
        pl.semaphore_signal(
            barrier, inc=1, device_id=(t // N_DST, t % N_DST), device_id_type=MESH
        )

    loop(DEVS - 1, greet)
    loads = [
        pltpu.make_async_copy(a, b, load_sem.at[i])
        for i, (a, b) in enumerate(
            [
                (state_in, state),
                (down_in, down),
                (dirs_in, dirs.at[s]),
                (edge_in, edge),
                (trip_in, trip),
                (mirror_in, mirror),
                (onehot_in, onehot),
                (pick_in, pick),
            ]
        )
    ]
    for load in loads:
        load.start()
    total[...] = jnp.zeros_like(total)
    arr[pl.ds(me, 1)] = jnp.zeros((1, CAP, WIDTH), BF16)

    def rows_of(ref, g):
        return ref[pl.ds(g * N_DST, N_DST)].reshape(CHUNK, WIDTH)

    def put_rows(ref, g, value):
        ref[pl.ds(g * N_DST, N_DST)] = value.reshape(N_DST, CAP, WIDTH)

    def live_of(g):
        return col[pl.ds(pl.multiple_of(g * CHUNK, CHUNK), CHUNK), 3:4]

    def lower(level, g, value):
        low = (silu(dot(value, down[level])) * live_of(g)).astype(BF16)
        low = low.reshape(BPC, 2, BLK // 2, TRIP)
        pool[pl.ds(s * NBLOCK + g * BPC, BPC)] = jnp.concatenate(
            [low[:, 0], low[:, 1]], axis=-1
        )

    def share(g, k):
        piece = pool.at[pl.ds(s * NBLOCK + g * BPC, BPC)]
        for hop in range(1, 4):
            remote(
                piece,
                piece,
                pool_send.at[hop - 1, k],
                pool_recv.at[s, k],
                ((x + hop) % 4) * 2 + core,
                d,
            ).start()
        remote(piece, piece, side_send.at[0, k], side_recv.at[x, k], twin, d).start()

    def forward(k):
        for hop in range(1, 4):
            owner = ((x + 4 - hop) % 4) * 2 + core
            piece = pool.at[pl.ds(owner * NBLOCK + k * BPC, BPC)]
            drain(piece, pool_recv.at[owner, k])
            remote(
                piece, piece, side_send.at[hop, k], side_recv.at[owner // 2, k], twin, d
            ).start()

    def settle(k):
        for hop in range(4):
            owner = ((x + hop) % 4) * 2 + (1 - core)
            piece = pool.at[pl.ds(owner * NBLOCK + k * BPC, BPC)]
            drain(piece, side_recv.at[owner // 2, k])
            drain(piece, side_send.at[hop, k])
        for hop in range(3):
            drain(piece, pool_send.at[hop, k])

    def base_of(level, g):
        base[pl.ds(pl.multiple_of(g * CHUNK, CHUNK), CHUNK), :] = dot(
            rows_of(state, g), edge[level, 0]
        )

    loads[0].wait()
    loads[1].wait()
    loads[2].wait()
    loop(N_SRC, lambda g: lower(0, g, rows_of(state, g)))
    pl.semaphore_wait(barrier, DEVS - 1)
    for hop in range(1, N_SRC):
        remote(
            dirs.at[s],
            dirs.at[s],
            dirs_send.at[hop],
            dirs_recv.at[s],
            (s + hop) % N_SRC,
            d,
        ).start()
    loop(N_SRC, lambda g: share(g, g))
    loads[3].wait()
    loop(N_SRC, lambda g: base_of(0, g))
    for load in loads[4:]:
        load.wait()
    for hop in range(1, N_SRC):
        drain(dirs.at[s], dirs_send.at[hop])
        owner = (s + hop) % N_SRC
        drain(dirs.at[owner], dirs_recv.at[owner])

    def angles(c):
        start = pl.multiple_of(c * BLK, BLK)
        mine = [
            jnp.broadcast_to(col[pl.ds(start, BLK), i : i + 1], (BLK, BLK)) for i in range(3)
        ]
        for q in range(PAIRS):
            pick_block = tri[c, q]
            other = dirs[pick_block // NBLOCK, pick_block % NBLOCK]
            cosine = mine[0] * other[0:1, :] + mine[1] * other[1:2, :] + mine[2] * other[2:3, :]
            square = cosine * cosine
            values = [
                cosine,
                1.5 * square - 0.5,
                (2.5 * square - 1.5) * cosine,
                (35.0 * square * square - 30.0 * square + 3.0) * 0.125,
            ]
            for i, value in enumerate(values):
                tiles[c, i * BLK : (i + 1) * BLK, q * BLK : (q + 1) * BLK] = value.astype(BF16)

    loop(NBLOCK, angles)

    def run_level(level):
        loop(N_SRC, forward)
        loop(N_SRC, settle)

        def talk(j):
            g = (s + 1 + j) % N_SRC
            parts = []
            for i in range(BPC):
                c = g * BPC + i
                chosen = []
                for q in range(PAIRS):
                    block = pool[tri[c, q]]
                    chosen += [block[:, :TRIP], block[:, TRIP:]]
                summed = dot(tiles[c], jnp.concatenate(chosen, axis=0))
                summed = (summed * (BLK * PAIRS) ** (-0.5)).astype(BF16)
                parts.append(
                    jnp.concatenate(
                        [summed[n * BLK : (n + 1) * BLK] for n in range(NSPH)], axis=1
                    )
                )
            triple = jnp.concatenate(parts, axis=0)
            pre = base[pl.ds(pl.multiple_of(g * CHUNK, CHUNK), CHUNK), :] + dot(
                triple, trip[level]
            )
            put_rows(msg, g, (silu(pre) * live_of(g)).astype(BF16))

            def send(i):
                t = (d + 1 + i) % N_DST
                b = g * N_DST + t

                @pl.when(b != me)
                def _():
                    remote(msg.at[b], arr.at[me], msg_send, msg_recv.at[s], g, t).start()

            loop(N_DST, send)

        loop(N_SRC, talk)

        def listen(j):
            g = (s + N_SRC - 1 - j) % N_SRC

            @pl.when(g != s)
            def _():
                drain(arr.at[pl.ds(g * N_DST, N_DST)], msg_recv.at[g])

            @pl.when(g == s)
            def _():
                drain(arr.at[pl.ds(0, N_DST - 1)], msg_recv.at[g])

            came = rows_of(arr, g)
            mirrored = jnp.concatenate(
                [
                    dot(mirror[g * BPC + i], came[i * BLK : (i + 1) * BLK])
                    for i in range(BPC)
                ],
                axis=0,
            )
            symmetric = (rows_of(msg, g).astype(F32) + mirrored).astype(BF16)
            inner = silu(dot(symmetric, edge[level, 1])).astype(BF16)
            value = (symmetric.astype(F32) + dot(inner, edge[level, 2])).astype(BF16)
            put_rows(refined, g, value)
            total[...] += dot(onehot[g], value)

        loop(N_SRC, listen)
        part[...] = total[...].astype(BF16).reshape(N_SRC, PIECE, WIDTH)
        for hop in range(1, N_SRC):
            t = (s + hop) % N_SRC
            remote(part.at[t], gathered.at[s], part_send.at[hop], part_recv.at[s], t, d).start()
        gathered[pl.ds(s, 1)] = part[pl.ds(s, 1)]
        total[...] = jnp.zeros_like(total)
        drain(arr.at[pl.ds(0, DEVS - 1)], msg_send)
        for hop in range(1, N_SRC):
            owner = (s + hop) % N_SRC
            drain(gathered.at[owner], part_recv.at[owner])
        sums = gathered[0].astype(F32)
        for i in range(1, N_SRC):
            sums += gathered[i].astype(F32)
        sums = (sums * DEGREE ** (-0.5)).astype(BF16)
        atoms[...] = sums
        home = d // 2
        slot = d % 2

        def spread(i):
            t = (d + 1 + i) % N_DST

            @pl.when(home * N_DST + t != me)
            def _():
                remote(
                    atoms, region.at[slot, s], atom_send, atom_recv, home, t
                ).start()

        loop(N_DST, spread)

        @pl.when(home == s)
        def _():
            region[pl.ds(slot, 1), pl.ds(s, 1)] = sums[None, None]
            drain(arr.at[pl.ds(0, 2 * (N_DST - 1))], atom_recv)
            drain(arr.at[pl.ds(0, 2 * (N_DST - 1))], atom_send)

        @pl.when(home != s)
        def _():
            drain(arr.at[pl.ds(0, 2 * N_DST)], atom_recv)
            drain(arr.at[pl.ds(0, 2 * N_DST)], atom_send)

        for hop in range(1, N_SRC):
            drain(part.at[0], part_send.at[hop])

        def update(g):
            value = rows_of(refined, g).astype(F32)
            feed = dot(pick[g], region[...].reshape(2 * ATOM_ROWS, WIDTH))
            joined = (value + feed).astype(BF16)
            first = silu(dot(joined, edge[level, 3])).astype(BF16)
            second = silu(dot(first, edge[level, 4])).astype(BF16)
            fresh = rows_of(state, g).astype(F32) + value + dot(second, edge[level, 5])
            fresh = (fresh * (live_of(g) * 0.5**0.5)).astype(BF16)
            put_rows(state, g, fresh)

            @pl.when(level < NBLK - 1)
            def _():
                lower(level + 1, g, fresh)
                share(g, g)

            @pl.when(level == NBLK - 1)
            def _():
                piece = pl.ds(g * N_DST, N_DST)
                pltpu.make_async_copy(state.at[piece], out.at[piece], out_sem).start()

        loop(N_SRC, update)

        @pl.when(level < NBLK - 1)
        def _():
            loop(N_SRC, lambda g: base_of(level + 1, g))

    loop(NBLK, run_level)
    drain(state, out_sem)


def body(
    edge_state, directions, src_atom, dst_atom, rev_pos, counts, triplets, down_w, trip_w, edge_w
):
    live = (jnp.arange(CAP)[None, :] < counts[0][:, None]).reshape(ROWS, 1)
    col = jnp.concatenate([directions.T, live.astype(F32)], axis=1)
    dirs = jnp.moveaxis(directions.reshape(3, NBLOCK, BLK), 0, 1)
    onehot = (
        dst_atom.reshape(N_SRC, 1, CHUNK) == jnp.arange(ATOM_ROWS, dtype=jnp.int32)[:, None]
    ).astype(BF16)
    slot = jnp.arange(ROWS, dtype=jnp.int32) % BLK
    target = (slot - slot % CAP + rev_pos).reshape(NBLOCK, BLK, 1)
    mirror = (
        (target == jnp.arange(BLK, dtype=jnp.int32)) & live.reshape(NBLOCK, BLK, 1)
    ).astype(BF16)
    pick = (
        src_atom.reshape(N_SRC, CHUNK, 1) == jnp.arange(2 * ATOM_ROWS, dtype=jnp.int32)
    ).astype(BF16)
    vmem = pl.BlockSpec(memory_space=pltpu.VMEM)
    hbm = pl.BlockSpec(memory_space=pl.ANY)
    dma = pltpu.SemaphoreType.DMA
    out = pl.pallas_call(
        kernel,
        out_shape=jax.ShapeDtypeStruct((DEVS, CAP, WIDTH), BF16),
        in_specs=[pl.BlockSpec(memory_space=pltpu.SMEM), vmem] + [hbm] * 8,
        out_specs=hbm,
        scratch_shapes=[
            pltpu.VMEM((DEVS, CAP, WIDTH), BF16),
            pltpu.VMEM((ROWS, WIDTH), F32),
            pltpu.VMEM((DEVS, CAP, WIDTH), BF16),
            pltpu.VMEM((DEVS, CAP, WIDTH), BF16),
            pltpu.VMEM((DEVS, CAP, WIDTH), BF16),
            pltpu.VMEM((NBLOCK, NSPH * BLK, PAIRS * BLK), BF16),
            pltpu.VMEM((N_SRC * NBLOCK, BLK // 2, 2 * TRIP), BF16),
            pltpu.VMEM((N_SRC, NBLOCK, 3, BLK), F32),
            pltpu.VMEM(onehot.shape, BF16),
            pltpu.VMEM(mirror.shape, BF16),
            pltpu.VMEM(pick.shape, BF16),
            pltpu.VMEM(down_w.shape, BF16),
            pltpu.VMEM(trip_w.shape, BF16),
            pltpu.VMEM(edge_w.shape, BF16),
            pltpu.VMEM((ATOM_ROWS, WIDTH), F32),
            pltpu.VMEM((N_SRC, PIECE, WIDTH), BF16),
            pltpu.VMEM((N_SRC, PIECE, WIDTH), BF16),
            pltpu.VMEM((PIECE, WIDTH), BF16),
            pltpu.VMEM((2, N_SRC, PIECE, WIDTH), BF16),
            dma((8,)),
            dma,
            dma((N_SRC,)),
            dma((N_SRC,)),
            dma((3, N_SRC)),
            dma((N_SRC, N_SRC)),
            dma((4, N_SRC)),
            dma((4, N_SRC)),
            dma,
            dma((N_SRC,)),
            dma((N_SRC,)),
            dma((N_SRC,)),
            dma,
            dma,
        ],
        compiler_params=pltpu.CompilerParams(
            collective_id=0, has_side_effects=True, vmem_limit_bytes=60 << 20
        ),
    )(
        triplets,
        col,
        dirs,
        edge_state.reshape(DEVS, CAP, WIDTH),
        onehot,
        mirror,
        pick,
        down_w,
        trip_w,
        edge_w,
    )
    return out.reshape(ROWS, WIDTH)


def solution(mesh):
    placed = (
        P(("src", "dst"), None),
        P(None, ("src", "dst")),
        P(("src", "dst")),
        P(("src", "dst")),
        P(("src", "dst")),
        P(("src", "dst"), None),
        P(("src", "dst"), None),
        P(),
        P(),
        P(),
    )
    return jax.shard_map(
        body, mesh=mesh, in_specs=placed, out_specs=P(("src", "dst"), None), check_vma=False
    )
```

profile of v0, /device:TPU:1, one launch (start us, length us, event | category | flops | bytes accessed | tf_op | source)
XLA Modules:
  0.0 202.5 jit_solution(10238728470187339010)
XLA Ops:
  0.0 0.5 broadcast.21
  0.5 1.3 reduce.3
  1.8 0.1 lt.59
  1.9 0.1 lt.61
  2.0 0.7 eq.56
  2.7 0.7 eq.48
  3.4 0.7 fusion.8
  4.1 1.4 copy.18.tri
  5.5 0.1 lt.62
  5.5 0.1 lt.63
  5.6 0.7 fusion.4
  6.4 0.1 reshape.66
  6.5 0.8 pad_maximum_fusion
  7.3 1.8 copy.20.down_in
  9.0 1.4 fusion.3.mirror_in
  10.4 1.4 copy.19.col
  11.8 1.3 fusion.1.onehot_in
  13.1 1.6 fusion.pick_in
  14.6 184.8 %shard_map.100 = bf16[128,16,512]{2,1,0:T(8,128)(2,1)} custom-call(s32[16,4]{1,0:T(8,128)} %copy.18.tri, f32[2048,4]{1,0:T(8,128)} %copy.19.col, f32[16,3,128]{2,1,0:T(4,128)} %bitcast.14, bf16[128,16,512]{2,1,0:T(8,128)(2,1)} %bitcast.12, bf16[8,256,256]{2,1,0:T(8,128)(2,1)} %fusion.1.onehot_in, bf16[16,128,128]{2,1,0:T(8,128)(2,1)} %fusion.3.mirror_in, ...), custom_call_target="tpu_custom_call" | custom-call | tf_op jit(solution)/shard_map/pallas_call | solution.py:396
  199.4 3.0 %copy.22 = bf16[2048,512]{1,0:T(8,128)(2,1)} copy(bf16[2048,512]{1,0:T(8,128)(2,1)} %bitcast.11) | data formatting | bytes 4194304
  (2 shorter events, 0.0 us)
where the time goes:
time: 203 us; the launch traced here: 202 us
  Pallas kernels  185 us (91%)
  local copies, waits for them, and re-layouts  9.84 us (5%)
  other arithmetic  7.81 us (4%)
    pallas_call x1, Pallas kernels, body(): pl.pallas_call(kernel, out_shape=jax.ShapeDtypeStruct((DEVS, CAP, WIDTH),...  185 us
    unnamed x4, local copies, waits for them, and re-layouts  6.66 us

commit v1 on v0

v1 whole, which is shorter than its diff:
```python
import jax
import jax.numpy as jnp
from jax import lax
from jax.experimental import pallas as pl
from jax.experimental.pallas import tpu as pltpu
from jax.sharding import PartitionSpec as P

BLK = 128
PAIRS = 4
NBLK = 2
HARM = 24
HPAD = 32
TRIP = 64
DEGREE = 64
N_SRC = 8
N_DST = 16
DEVS = N_SRC * N_DST
CAP = 16
WIDTH = 512
ROWS = DEVS * CAP
CHUNK = N_DST * CAP
NBLOCK = ROWS // BLK
BPC = CHUNK // BLK
ATOM_ROWS = 256
PIECE = ATOM_ROWS // N_SRC
MESH = pl.DeviceIdType.MESH
F32 = jnp.float32
BF16 = jnp.bfloat16


def silu(value):
    half = 0.5 * value
    return half + half * jnp.tanh(half)


def dot(a, b):
    return jnp.dot(a, b, preferred_element_type=F32)


def loop(count, step):
    def body(i, carry):
        step(i)
        return carry

    lax.fori_loop(0, count, body, 0)


def harmonics(x, y, z):
    xx, yy, zz = x * x, y * y, z * z
    diff = xx - yy
    r3, r5, r15, r35 = 3.0**0.5, 5.0**0.5, 15.0**0.5, 35.0**0.5
    r38, r58, r358 = 0.375**0.5, 0.625**0.5, 4.375**0.5
    return [
        x,
        y,
        z,
        r3 * x * y,
        r3 * y * z,
        r3 * x * z,
        0.5 * r3 * diff,
        1.5 * zz - 0.5,
        r58 * y * (3.0 * xx - yy),
        r15 * x * y * z,
        r38 * y * (5.0 * zz - 1.0),
        0.5 * z * (5.0 * zz - 3.0),
        r38 * x * (5.0 * zz - 1.0),
        0.5 * r15 * z * diff,
        r58 * x * (xx - 3.0 * yy),
        0.5 * r35 * x * y * diff,
        r358 * y * z * (3.0 * xx - yy),
        0.5 * r5 * x * y * (7.0 * zz - 1.0),
        r58 * y * z * (7.0 * zz - 3.0),
        0.125 * (35.0 * zz * zz - 30.0 * zz + 3.0),
        r58 * x * z * (7.0 * zz - 3.0),
        0.25 * r5 * diff * (7.0 * zz - 1.0),
        r358 * x * z * (xx - 3.0 * yy),
        0.125 * r35 * (xx * xx - 6.0 * xx * yy + yy * yy),
    ]


def kernel(
    tri,
    dirs_in,
    src_in,
    dst_in,
    rev_in,
    counts_in,
    state_in,
    down_in,
    trip_in,
    edge_in,
    out,
    state,
    base,
    msg,
    arr,
    refined,
    split,
    field,
    rows_y,
    cols,
    pool,
    spectrum,
    lifted,
    onehot,
    mirror,
    pick,
    down,
    trip,
    edge,
    total,
    part,
    gathered,
    atoms,
    region,
    load_sem,
    out_sem,
    pool_send,
    pool_recv,
    msg_send,
    msg_recv,
    part_send,
    part_recv,
    atom_send,
    atom_recv,
):
    s = lax.axis_index("src")
    d = lax.axis_index("dst")
    me = s * N_DST + d
    x = s // 2
    z = d // 4
    y = d % 4

    def remote(src, dst, send, recv, ts, td):
        return pltpu.make_async_remote_copy(
            src_ref=src,
            dst_ref=dst,
            send_sem=send,
            recv_sem=recv,
            device_id=(ts, td),
            device_id_type=MESH,
        )

    def drain(ref, sem):
        pltpu.make_async_copy(ref, ref, sem).wait()

    barrier = pltpu.get_barrier_semaphore()

    def greet(i):
        t = (me + 1 + i) % DEVS
        pl.semaphore_signal(
            barrier, inc=1, device_id=(t // N_DST, t % N_DST), device_id_type=MESH
        )

    loop(DEVS - 1, greet)
    loads = [
        pltpu.make_async_copy(a, b, load_sem.at[i])
        for i, (a, b) in enumerate(
            [(state_in, state), (down_in, down), (edge_in, edge), (trip_in, trip)]
        )
    ]
    for load in loads:
        load.start()
    total[...] = jnp.zeros_like(total)
    arr[pl.ds(me, 1)] = jnp.zeros((1, CAP, WIDTH), BF16)

    def iota(shape, axis):
        return lax.broadcasted_iota(jnp.int32, shape, axis)

    lane = iota((NBLOCK, BLK), 1)
    number = iota((NBLOCK, BLK), 0)
    spread_counts = jnp.where(
        lane // (BLK // CAP) == number,
        jnp.broadcast_to(counts_in[...], (NBLOCK, BLK)),
        0,
    ).astype(F32)
    widen = iota((BLK, BLK), 0) % (BLK // CAP) == iota((BLK, BLK), 1) // CAP
    filled = dot(spread_counts.astype(BF16), widen.astype(F32).astype(BF16))
    slot = lane % CAP
    for c in range(NBLOCK):
        split[c, 0:3, :] = dirs_in[:, c * BLK : (c + 1) * BLK]
    field[...] = jnp.zeros_like(field)
    planes = harmonics(split[:, 0, :], split[:, 1, :], split[:, 2, :])
    for i, plane in enumerate(planes):
        field[:, i, :] = plane
    rows_y[...] = field[...].astype(BF16)
    field[:, HARM, :] = (slot.astype(F32) < filled).astype(F32)
    field[:, HARM + 1, :] = src_in[...].astype(F32)
    field[:, HARM + 2, :] = (lane - slot + rev_in[...]).astype(F32)

    def turn(c):
        cols[c] = field[c].T

    loop(NBLOCK, turn)

    def rows_of(ref, g):
        return ref[pl.ds(g * N_DST, N_DST)].reshape(CHUNK, WIDTH)

    def put_rows(ref, g, value):
        ref[pl.ds(g * N_DST, N_DST)] = value.reshape(N_DST, CAP, WIDTH)

    def live_of(g):
        return cols[pl.ds(g * BPC, BPC), :, HARM : HARM + 1].reshape(CHUNK, 1)

    def lower(level, g, value):
        low = lax.dot_general(
            value, down[level], (((1,), (1,)), ((), ())), preferred_element_type=F32
        )
        low = (silu(low) * live_of(g)).astype(BF16)
        for i in range(BPC):
            c = g * BPC + i
            modes = dot(rows_y[c], low[i * BLK : (i + 1) * BLK])
            pool[s * NBLOCK + c] = jnp.concatenate(
                [modes[: HPAD // 2], modes[HPAD // 2 :]], axis=1
            ).astype(BF16)

    def share(start, count):
        piece = pool.at[pl.ds(s * NBLOCK + start, count)]
        for hop in range(1, N_SRC):
            remote(
                piece, piece, pool_send, pool_recv.at[s], (s + hop) % N_SRC, d
            ).start()

    def span(g):
        return pl.ds(pl.multiple_of(g * CHUNK, CHUNK), CHUNK)

    def base_of(level, g):
        base[span(g), :] = dot(rows_of(state, g), edge[level, 0])

    loads[0].wait()
    loads[1].wait()
    loop(N_SRC, lambda g: lower(0, g, rows_of(state, g)))
    pl.semaphore_wait(barrier, DEVS - 1)
    share(0, NBLOCK)

    def choose(c):
        column = cols[c]
        source = column[:, HARM + 1 : HARM + 2]
        target = column[:, HARM + 2 : HARM + 3]
        alive = column[:, HARM : HARM + 1]
        pick[c] = (source == iota((BLK, 2 * ATOM_ROWS), 1).astype(F32)).astype(F32).astype(BF16)
        same = (target == iota((BLK, BLK), 1).astype(F32)).astype(F32)
        mirror[c] = (same * alive).astype(BF16)
        onehot[c] = (
            (iota((ATOM_ROWS, BLK), 0) == dst_in[pl.ds(c, 1), :]).astype(F32).astype(BF16)
        )

    loop(NBLOCK, choose)
    loads[2].wait()
    loop(N_SRC, lambda g: base_of(0, g))
    loads[3].wait()
    mode = iota((HPAD, 4 * TRIP), 0)
    degree = (
        (mode >= 3).astype(jnp.int32)
        + (mode >= 8).astype(jnp.int32)
        + (mode >= 15).astype(jnp.int32)
    )
    keep = (degree == iota((HPAD, 4 * TRIP), 1) // TRIP).astype(F32) * (BLK * PAIRS) ** (-0.5)

    def run_level(level):
        drain(pool.at[pl.ds(0, (N_SRC - 1) * NBLOCK)], pool_send)
        for hop in range(1, N_SRC):
            owner = (s + hop) % N_SRC
            drain(pool.at[pl.ds(owner * NBLOCK, NBLOCK)], pool_recv.at[owner])

        def mix(c):
            modes = pool[tri[0, c]].astype(F32)
            for q in range(1, PAIRS):
                modes += pool[tri[q, c]].astype(F32)
            modes = jnp.concatenate([modes[:, :TRIP], modes[:, TRIP:]], axis=0)
            spectrum[c] = (jnp.concatenate([modes] * 4, axis=1) * keep).astype(BF16)

        loop(NBLOCK, mix)
        lifted[...] = (
            dot(spectrum[...].reshape(NBLOCK * HPAD, 4 * TRIP), trip[level])
            .astype(BF16)
            .reshape(NBLOCK, HPAD, WIDTH)
        )

        def talk(j):
            g = (s + 1 + j) % N_SRC
            parts = [
                dot(cols[g * BPC + i].astype(BF16), lifted[g * BPC + i]) for i in range(BPC)
            ]
            pre = base[span(g), :] + jnp.concatenate(parts, axis=0)
            put_rows(msg, g, (silu(pre) * live_of(g)).astype(BF16))

            def send(i):
                t = (d + 1 + i) % N_DST
                b = g * N_DST + t

                @pl.when(b != me)
                def _():
                    remote(msg.at[b], arr.at[me], msg_send, msg_recv.at[s], g, t).start()

            loop(N_DST, send)

        loop(N_SRC, talk)

        def listen(j):
            g = (s + N_SRC - 1 - j) % N_SRC

            @pl.when(g != s)
            def _():
                drain(arr.at[pl.ds(g * N_DST, N_DST)], msg_recv.at[g])

            @pl.when(g == s)
            def _():
                drain(arr.at[pl.ds(0, N_DST - 1)], msg_recv.at[g])

            came = rows_of(arr, g)
            mirrored = jnp.concatenate(
                [
                    dot(mirror[g * BPC + i], came[i * BLK : (i + 1) * BLK])
                    for i in range(BPC)
                ],
                axis=0,
            )
            symmetric = (rows_of(msg, g).astype(F32) + mirrored).astype(BF16)
            inner = silu(dot(symmetric, edge[level, 1])).astype(BF16)
            value = (symmetric.astype(F32) + dot(inner, edge[level, 2])).astype(BF16)
            put_rows(refined, g, value)
            sums = total[...]
            for i in range(BPC):
                sums += dot(onehot[g * BPC + i], value[i * BLK : (i + 1) * BLK])
            total[...] = sums
            base[span(g), :] = dot(value, edge[level, 3])

        loop(N_SRC, listen)
        part[...] = total[...].astype(BF16).reshape(N_SRC, PIECE, WIDTH)
        for hop in range(N_SRC):
            t = (s + hop) % N_SRC
            td = ((z + t // 2) % 4) * 4 + y

            @pl.when((t != s) | (td != d))
            def _():
                remote(
                    part.at[t], gathered.at[s], part_send, part_recv, t, td
                ).start()

        home = ((z + 4 - x) % 4) * 4 + y
        total[...] = jnp.zeros_like(total)
        drain(arr.at[pl.ds(0, DEVS - 1)], msg_send)

        @pl.when(home == d)
        def _():
            gathered[pl.ds(s, 1)] = part[pl.ds(s, 1)]
            drain(gathered.at[pl.ds(0, N_SRC - 1)], part_recv)
            drain(gathered.at[pl.ds(0, N_SRC - 1)], part_send)

        @pl.when(home != d)
        def _():
            drain(gathered, part_recv)
            drain(gathered, part_send)

        sums = gathered[0].astype(F32)
        for i in range(1, N_SRC):
            sums += gathered[i].astype(F32)
        sums = (sums * DEGREE ** (-0.5)).astype(BF16)
        atoms[...] = sums
        near = home // 2
        slot = home % 2

        def spread(i):
            t = (d + 1 + i) % N_DST

            @pl.when(near * N_DST + t != me)
            def _():
                remote(atoms, region.at[slot, s], atom_send, atom_recv, near, t).start()

        loop(N_DST, spread)

        @pl.when(near == s)
        def _():
            region[pl.ds(slot, 1), pl.ds(s, 1)] = sums[None, None]
            drain(arr.at[pl.ds(0, 2 * (N_DST - 1))], atom_recv)
            drain(arr.at[pl.ds(0, 2 * (N_DST - 1))], atom_send)

        @pl.when(near != s)
        def _():
            drain(arr.at[pl.ds(0, 2 * N_DST)], atom_recv)
            drain(arr.at[pl.ds(0, 2 * N_DST)], atom_send)

        known = dot(region[...].reshape(2 * ATOM_ROWS, WIDTH), edge[level, 3]).astype(BF16)
        region[...] = known.reshape(region.shape)

        def update(g):
            chosen = pick[pl.ds(g * BPC, BPC)].reshape(CHUNK, 2 * ATOM_ROWS)
            feed = dot(chosen, region[...].reshape(2 * ATOM_ROWS, WIDTH))
            first = silu(base[span(g), :] + feed).astype(BF16)
            second = silu(dot(first, edge[level, 4])).astype(BF16)
            fresh = (
                rows_of(state, g).astype(F32)
                + rows_of(refined, g).astype(F32)
                + dot(second, edge[level, 5])
            )
            fresh = (fresh * (live_of(g) * 0.5**0.5)).astype(BF16)
            put_rows(state, g, fresh)

            @pl.when(level < NBLK - 1)
            def _():
                lower(level + 1, g, fresh)
                share(g * BPC, BPC)

            @pl.when(level == NBLK - 1)
            def _():
                piece = pl.ds(g * N_DST, N_DST)
                pltpu.make_async_copy(state.at[piece], out.at[piece], out_sem).start()

        loop(N_SRC, update)

        @pl.when(level < NBLK - 1)
        def _():
            loop(N_SRC, lambda g: base_of(level + 1, g))

    loop(NBLK, run_level)
    drain(state, out_sem)


def body(
    edge_state, directions, src_atom, dst_atom, rev_pos, counts, triplets, down_w, trip_w, edge_w
):
    vmem = pl.BlockSpec(memory_space=pltpu.VMEM)
    hbm = pl.BlockSpec(memory_space=pl.ANY)
    dma = pltpu.SemaphoreType.DMA
    down = jnp.swapaxes(down_w, 1, 2)
    edges = pltpu.VMEM((DEVS, CAP, WIDTH), BF16)
    out = pl.pallas_call(
        kernel,
        out_shape=jax.ShapeDtypeStruct((DEVS, CAP, WIDTH), BF16),
        in_specs=[pl.BlockSpec(memory_space=pltpu.SMEM)] + [vmem] * 5 + [hbm] * 4,
        out_specs=hbm,
        scratch_shapes=[
            edges,
            pltpu.VMEM((ROWS, WIDTH), F32),
            edges,
            edges,
            edges,
            pltpu.VMEM((NBLOCK, 8, BLK), F32),
            pltpu.VMEM((NBLOCK, HPAD, BLK), F32),
            pltpu.VMEM((NBLOCK, HPAD, BLK), BF16),
            pltpu.VMEM((NBLOCK, BLK, HPAD), F32),
            pltpu.VMEM((N_SRC * NBLOCK, HPAD // 2, 2 * TRIP), BF16),
            pltpu.VMEM((NBLOCK, HPAD, 4 * TRIP), BF16),
            pltpu.VMEM((NBLOCK, HPAD, WIDTH), BF16),
            pltpu.VMEM((NBLOCK, ATOM_ROWS, BLK), BF16),
            pltpu.VMEM((NBLOCK, BLK, BLK), BF16),
            pltpu.VMEM((NBLOCK, BLK, 2 * ATOM_ROWS), BF16),
            pltpu.VMEM(down.shape, BF16),
            pltpu.VMEM(trip_w.shape, BF16),
            pltpu.VMEM(edge_w.shape, BF16),
            pltpu.VMEM((ATOM_ROWS, WIDTH), F32),
            pltpu.VMEM((N_SRC, PIECE, WIDTH), BF16),
            pltpu.VMEM((N_SRC, PIECE, WIDTH), BF16),
            pltpu.VMEM((PIECE, WIDTH), BF16),
            pltpu.VMEM((2, N_SRC, PIECE, WIDTH), BF16),
            dma((4,)),
            dma,
            dma,
            dma((N_SRC,)),
            dma,
            dma((N_SRC,)),
            dma,
            dma,
            dma,
            dma,
        ],
        compiler_params=pltpu.CompilerParams(
            collective_id=0, has_side_effects=True, vmem_limit_bytes=60 << 20
        ),
    )(
        triplets.T,
        directions,
        src_atom.reshape(NBLOCK, BLK),
        dst_atom.reshape(NBLOCK, BLK),
        rev_pos.reshape(NBLOCK, BLK),
        counts,
        edge_state.reshape(DEVS, CAP, WIDTH),
        down,
        trip_w,
        edge_w,
    )
    return out.reshape(ROWS, WIDTH)


def solution(mesh):
    placed = (
        P(("src", "dst"), None),
        P(None, ("src", "dst")),
        P(("src", "dst")),
        P(("src", "dst")),
        P(("src", "dst")),
        P(("src", "dst"), None),
        P(("src", "dst"), None),
        P(),
        P(),
        P(),
    )
    return jax.shard_map(
        body, mesh=mesh, in_specs=placed, out_specs=P(("src", "dst"), None), check_vma=False
    )
```

time: 203 us -> 153 us (0.75)
  Pallas kernels: 185 us -> 148 us
  other arithmetic: 7.81 us -> 0 us
  local copies, waits for them, and re-layouts: 9.84 us -> 3.05 us
    pallas_call x1, Pallas kernels: 185 us -> 148 us  [body(): pl.pallas_call(kernel, out_shape=jax.ShapeDtypeStruct((DEVS, CAP, WIDTH),...]
    convert_element_type x4 -> x0, other arithmetic: 5.01 us -> none  [the longest x1 1.55 us: body(): pick = (src_atom.reshape(N_SRC, CHUNK, 1) == jnp.arange(2 * ATOM_ROWS, dt...]
    unnamed x4 -> x1, local copies, waits for them, and re-layouts: 6.66 us -> 3.05 us
where the time goes in v1:
time: 153 us; the launch traced here: 151 us
  Pallas kernels  148 us (97%)
  local copies, waits for them, and re-layouts  3.05 us (2%)
    pallas_call x1, Pallas kernels, body(): pl.pallas_call(kernel, out_shape=jax.ShapeDtypeStruct((DEVS, CAP, WIDTH),...  148 us

profile of v1, /device:TPU:1, one launch (start us, length us, event | category | flops | bytes accessed | tf_op | source)
XLA Modules:
  0.0 150.9 jit_solution(13274674489070268999)
XLA Ops:
  0.0 147.8 %shard_map.100 = bf16[128,16,512]{2,1,0:T(8,128)(2,1)} custom-call(s32[4,16]{1,0:T(4,128)} %bitcast.13, f32[3,2048]{1,0:T(4,128)} %dirs_in.1, s32[16,128]{1,0:T(8,128)} %bitcast.10, s32[16,128]{1,0:T(8,128)} %bitcast.11, s32[16,128]{1,0:T(8,128)} %bitcast.12, s32[1,128]{1,0:T(1,128)} %counts_in.1, bf16[128,16,512]{2,1,0:T(8,128)(2,1)} %bitcast.8, ...), custom_call_target="tpu_custom_call" | custom-call | tf_op jit(solution)/shard_map/pallas_call | solution.py:428
  147.9 3.0 %copy.12 = bf16[2048,512]{1,0:T(8,128)(2,1)} copy(bf16[2048,512]{1,0:T(8,128)(2,1)} %bitcast.7) | data formatting | bytes 4194304

commit v2 on v1

--- a/solution.py
+++ b/solution.py
@@ -21,8 +21,14 @@
 CHUNK = N_DST * CAP
 NBLOCK = ROWS // BLK
 BPC = CHUNK // BLK
+MIX = 4
+WIDE = 2
 ATOM_ROWS = 256
 PIECE = ATOM_ROWS // N_SRC
+FAR = sorted(
+    ((i, j) for i in range(4) for j in range(4)),
+    key=lambda p: -min(p[0], 4 - p[0]) - min(p[1], 4 - p[1]),
+)
 MESH = pl.DeviceIdType.MESH
 F32 = jnp.float32
 BF16 = jnp.bfloat16
@@ -128,6 +134,7 @@
     d = lax.axis_index("dst")
     me = s * N_DST + d
     x = s // 2
+    core = s % 2
     z = d // 4
     y = d % 4
 
@@ -146,13 +153,6 @@
 
     barrier = pltpu.get_barrier_semaphore()
 
-    def greet(i):
-        t = (me + 1 + i) % DEVS
-        pl.semaphore_signal(
-            barrier, inc=1, device_id=(t // N_DST, t % N_DST), device_id_type=MESH
-        )
-
-    loop(DEVS - 1, greet)
     loads = [
         pltpu.make_async_copy(a, b, load_sem.at[i])
         for i, (a, b) in enumerate(
@@ -161,6 +161,19 @@
     ]
     for load in loads:
         load.start()
+    def signal(ts, td):
+        pl.semaphore_signal(barrier, inc=1, device_id=(ts, td), device_id_type=MESH)
+
+    lines = [(s + hop) % N_SRC for hop in range(N_SRC)]
+
+    def greet(i):
+        td = (d + 1 + i) % N_DST
+        for ts in lines:
+            signal(ts, td)
+
+    loop(N_DST - 1, greet)
+    for ts in lines[1:]:
+        signal(ts, d)
     total[...] = jnp.zeros_like(total)
     arr[pl.ds(me, 1)] = jnp.zeros((1, CAP, WIDTH), BF16)
 
@@ -193,22 +206,24 @@
 
     loop(NBLOCK, turn)
 
-    def rows_of(ref, g):
-        return ref[pl.ds(g * N_DST, N_DST)].reshape(CHUNK, WIDTH)
-
-    def put_rows(ref, g, value):
-        ref[pl.ds(g * N_DST, N_DST)] = value.reshape(N_DST, CAP, WIDTH)
-
-    def live_of(g):
-        return cols[pl.ds(g * BPC, BPC), :, HARM : HARM + 1].reshape(CHUNK, 1)
+    def rows_of(ref, g, n=1):
+        return ref[pl.ds(g * n * N_DST, n * N_DST)].reshape(n * CHUNK, WIDTH)
+
+    def put_rows(ref, g, value, n=1):
+        ref[pl.ds(g * n * N_DST, n * N_DST)] = value.reshape(n * N_DST, CAP, WIDTH)
+
+    def live_of(g, n=1):
+        column = cols[pl.ds(g * n * BPC, n * BPC), :, HARM : HARM + 1]
+        return column.reshape(n * CHUNK, 1)
 
     def lower(level, g, value):
+        n = value.shape[0] // CHUNK
         low = lax.dot_general(
             value, down[level], (((1,), (1,)), ((), ())), preferred_element_type=F32
         )
-        low = (silu(low) * live_of(g)).astype(BF16)
-        for i in range(BPC):
-            c = g * BPC + i
+        low = (silu(low) * live_of(g, n)).astype(BF16)
+        for i in range(n * BPC):
+            c = g * n * BPC + i
             modes = dot(rows_y[c], low[i * BLK : (i + 1) * BLK])
             pool[s * NBLOCK + c] = jnp.concatenate(
                 [modes[: HPAD // 2], modes[HPAD // 2 :]], axis=1
@@ -221,8 +236,8 @@
                 piece, piece, pool_send, pool_recv.at[s], (s + hop) % N_SRC, d
             ).start()
 
-    def span(g):
-        return pl.ds(pl.multiple_of(g * CHUNK, CHUNK), CHUNK)
+    def span(g, n=1):
+        return pl.ds(pl.multiple_of(g * n * CHUNK, CHUNK), n * CHUNK)
 
     def base_of(level, g):
         base[span(g), :] = dot(rows_of(state, g), edge[level, 0])
@@ -263,14 +278,17 @@
             owner = (s + hop) % N_SRC
             drain(pool.at[pl.ds(owner * NBLOCK, NBLOCK)], pool_recv.at[owner])
 
-        def mix(c):
-            modes = pool[tri[0, c]].astype(F32)
-            for q in range(1, PAIRS):
-                modes += pool[tri[q, c]].astype(F32)
-            modes = jnp.concatenate([modes[:, :TRIP], modes[:, TRIP:]], axis=0)
-            spectrum[c] = (jnp.concatenate([modes] * 4, axis=1) * keep).astype(BF16)
-
-        loop(NBLOCK, mix)
+        def mix(i):
+            mixed = []
+            for k in range(MIX):
+                c = i * MIX + k
+                modes = [pool[tri[q, c]].astype(F32) for q in range(PAIRS)]
+                modes = (modes[0] + modes[1]) + (modes[2] + modes[3])
+                modes = jnp.concatenate([modes[:, :TRIP], modes[:, TRIP:]], axis=0)
+                mixed.append((jnp.concatenate([modes] * 4, axis=1) * keep).astype(BF16))
+            spectrum[pl.ds(i * MIX, MIX)] = jnp.stack(mixed)
+
+        loop(NBLOCK // MIX, mix)
         lifted[...] = (
             dot(spectrum[...].reshape(NBLOCK * HPAD, 4 * TRIP), trip[level])
             .astype(BF16)
@@ -286,14 +304,15 @@
             put_rows(msg, g, (silu(pre) * live_of(g)).astype(BF16))
 
             def send(i):
-                t = (d + 1 + i) % N_DST
-                b = g * N_DST + t
-
-                @pl.when(b != me)
-                def _():
-                    remote(msg.at[b], arr.at[me], msg_send, msg_recv.at[s], g, t).start()
-
-            loop(N_DST, send)
+                for k in range(4):
+                    t = (d + 1 + i * 4 + k) % N_DST
+                    b = g * N_DST + t
+
+                    @pl.when(b != me)
+                    def _():
+                        remote(msg.at[b], arr.at[me], msg_send, msg_recv.at[s], g, t).start()
+
+            loop(N_DST // 4, send)
 
         loop(N_SRC, talk)
 
@@ -324,13 +343,12 @@
             for i in range(BPC):
                 sums += dot(onehot[g * BPC + i], value[i * BLK : (i + 1) * BLK])
             total[...] = sums
-            base[span(g), :] = dot(value, edge[level, 3])
 
         loop(N_SRC, listen)
         part[...] = total[...].astype(BF16).reshape(N_SRC, PIECE, WIDTH)
         for hop in range(N_SRC):
             t = (s + hop) % N_SRC
-            td = ((z + t // 2) % 4) * 4 + y
+            td = ((z + t // 2 + 2 * (t % 2)) % 4) * 4 + y
 
             @pl.when((t != s) | (td != d))
             def _():
@@ -338,7 +356,11 @@
                     part.at[t], gathered.at[s], part_send, part_recv, t, td
                 ).start()
 
-        home = ((z + 4 - x) % 4) * 4 + y
+        def ahead(g):
+            base[span(g), :] = dot(rows_of(refined, g), edge[level, 3])
+
+        loop(N_SRC, ahead)
+        home = ((z + 8 - x - 2 * core) % 4) * 4 + y
         total[...] = jnp.zeros_like(total)
         drain(arr.at[pl.ds(0, DEVS - 1)], msg_send)
 
@@ -361,14 +383,12 @@
         near = home // 2
         slot = home % 2
 
-        def spread(i):
-            t = (d + 1 + i) % N_DST
+        for far in FAR:
+            t = ((z + far[0]) % 4) * 4 + (y + far[1]) % 4
 
             @pl.when(near * N_DST + t != me)
             def _():
                 remote(atoms, region.at[slot, s], atom_send, atom_recv, near, t).start()
-
-        loop(N_DST, spread)
 
         @pl.when(near == s)
         def _():
@@ -385,29 +405,30 @@
         region[...] = known.reshape(region.shape)
 
         def update(g):
-            chosen = pick[pl.ds(g * BPC, BPC)].reshape(CHUNK, 2 * ATOM_ROWS)
+            chosen = pick[pl.ds(g * WIDE * BPC, WIDE * BPC)]
+            chosen = chosen.reshape(WIDE * CHUNK, 2 * ATOM_ROWS)
             feed = dot(chosen, region[...].reshape(2 * ATOM_ROWS, WIDTH))
-            first = silu(base[span(g), :] + feed).astype(BF16)
+            first = silu(base[span(g, WIDE), :] + feed).astype(BF16)
             second = silu(dot(first, edge[level, 4])).astype(BF16)
             fresh = (
-                rows_of(state, g).astype(F32)
-                + rows_of(refined, g).astype(F32)
+                rows_of(state, g, WIDE).astype(F32)
+                + rows_of(refined, g, WIDE).astype(F32)
                 + dot(second, edge[level, 5])
             )
-            fresh = (fresh * (live_of(g) * 0.5**0.5)).astype(BF16)
-            put_rows(state, g, fresh)
+            fresh = (fresh * (live_of(g, WIDE) * 0.5**0.5)).astype(BF16)
+            put_rows(state, g, fresh, WIDE)
 
             @pl.when(level < NBLK - 1)
             def _():
                 lower(level + 1, g, fresh)
-                share(g * BPC, BPC)
+                share(g * WIDE * BPC, WIDE * BPC)
 
             @pl.when(level == NBLK - 1)
             def _():
-                piece = pl.ds(g * N_DST, N_DST)
+                piece = pl.ds(g * WIDE * N_DST, WIDE * N_DST)
                 pltpu.make_async_copy(state.at[piece], out.at[piece], out_sem).start()
 
-        loop(N_SRC, update)
+        loop(N_SRC // WIDE, update)
 
         @pl.when(level < NBLK - 1)
         def _():

time: 153 us -> 134 us (0.88); the launches traced: 151 us -> 134 us
  Pallas kernels: 148 us -> 131 us
    pallas_call x1, Pallas kernels: 148 us -> 131 us  [body(): pl.pallas_call(kernel, out_shape=jax.ShapeDtypeStruct((DEVS, CAP, WIDTH),...]
where the time goes in v2:
time: 134 us
  Pallas kernels  131 us (98%)
  local copies, waits for them, and re-layouts  3.05 us (2%)
    pallas_call x1, Pallas kernels, body(): pl.pallas_call(kernel, out_shape=jax.ShapeDtypeStruct((DEVS, CAP, WIDTH),...  131 us
    unnamed x1, local copies, waits for them, and re-layouts  3.05 us

profile of v2, /device:TPU:1, one launch (start us, length us, event | category | flops | bytes accessed | tf_op | source)
XLA Modules:
  0.0 134.1 jit_solution(12919998793530956343)
XLA Ops:
  0.0 131.0 %shard_map.100 = bf16[128,16,512]{2,1,0:T(8,128)(2,1)} custom-call(s32[4,16]{1,0:T(4,128)} %bitcast.13, f32[3,2048]{1,0:T(4,128)} %dirs_in.1, s32[16,128]{1,0:T(8,128)} %bitcast.10, s32[16,128]{1,0:T(8,128)} %bitcast.11, s32[16,128]{1,0:T(8,128)} %bitcast.12, s32[1,128]{1,0:T(1,128)} %counts_in.1, bf16[128,16,512]{2,1,0:T(8,128)(2,1)} %bitcast.8, ...), custom_call_target="tpu_custom_call" | custom-call | tf_op jit(solution)/shard_map/pallas_call | solution.py:449
  131.0 3.0 %copy.12 = bf16[2048,512]{1,0:T(8,128)(2,1)} copy(bf16[2048,512]{1,0:T(8,128)(2,1)} %bitcast.7) | data formatting | bytes 4194304

commit v3 on v2

--- a/solution.py
+++ b/solution.py
@@ -34,8 +34,7 @@
 BF16 = jnp.bfloat16
 
 
-def silu(value):
-    half = 0.5 * value
+def silu_of_half(half):
     return half + half * jnp.tanh(half)
 
 
@@ -95,7 +94,6 @@
     down_in,
     trip_in,
     edge_in,
-    out,
     state,
     base,
     msg,
@@ -120,7 +118,6 @@
     atoms,
     region,
     load_sem,
-    out_sem,
     pool_send,
     pool_recv,
     msg_send,
@@ -221,16 +218,18 @@
         low = lax.dot_general(
             value, down[level], (((1,), (1,)), ((), ())), preferred_element_type=F32
         )
-        low = (silu(low) * live_of(g, n)).astype(BF16)
+        low = (silu_of_half(low) * live_of(g, n)).astype(BF16)
+        modes = []
         for i in range(n * BPC):
             c = g * n * BPC + i
-            modes = dot(rows_y[c], low[i * BLK : (i + 1) * BLK])
-            pool[s * NBLOCK + c] = jnp.concatenate(
-                [modes[: HPAD // 2], modes[HPAD // 2 :]], axis=1
+            modes.append(dot(rows_y[c], low[i * BLK : (i + 1) * BLK])[:HARM])
+        for i in range(n):
+            pool[s * N_SRC + g * n + i] = jnp.concatenate(
+                [modes[2 * i], modes[2 * i + 1]], axis=1
             ).astype(BF16)
 
     def share(start, count):
-        piece = pool.at[pl.ds(s * NBLOCK + start, count)]
+        piece = pool.at[pl.ds(s * N_SRC + start, count)]
         for hop in range(1, N_SRC):
             remote(
                 piece, piece, pool_send, pool_recv.at[s], (s + hop) % N_SRC, d
@@ -244,9 +243,10 @@
 
     loads[0].wait()
     loads[1].wait()
+    down[...] = down[...] * 0.5
     loop(N_SRC, lambda g: lower(0, g, rows_of(state, g)))
     pl.semaphore_wait(barrier, DEVS - 1)
-    share(0, NBLOCK)
+    share(0, N_SRC)
 
     def choose(c):
         column = cols[c]
@@ -261,31 +261,45 @@
         )
 
     loop(NBLOCK, choose)
+
+    def halve(level):
+        for i in (0, 1, 3, 4):
+            edge[level, i] = edge[level, i] * 0.5
+
     loads[2].wait()
+    loop(NBLK, halve)
     loop(N_SRC, lambda g: base_of(0, g))
     loads[3].wait()
-    mode = iota((HPAD, 4 * TRIP), 0)
+    mode = iota((HARM, 4 * TRIP), 0)
     degree = (
         (mode >= 3).astype(jnp.int32)
         + (mode >= 8).astype(jnp.int32)
         + (mode >= 15).astype(jnp.int32)
     )
-    keep = (degree == iota((HPAD, 4 * TRIP), 1) // TRIP).astype(F32) * (BLK * PAIRS) ** (-0.5)
+    keep = (degree == iota((HARM, 4 * TRIP), 1) // TRIP).astype(F32) * (0.5 * (BLK * PAIRS) ** (-0.5))
+
+    side = iota((HARM, 2 * TRIP), 1) // TRIP
 
     def run_level(level):
-        drain(pool.at[pl.ds(0, (N_SRC - 1) * NBLOCK)], pool_send)
+        drain(pool.at[pl.ds(0, (N_SRC - 1) * N_SRC)], pool_send)
         for hop in range(1, N_SRC):
             owner = (s + hop) % N_SRC
-            drain(pool.at[pl.ds(owner * NBLOCK, NBLOCK)], pool_recv.at[owner])
+            drain(pool.at[pl.ds(owner * N_SRC, N_SRC)], pool_recv.at[owner])
 
         def mix(i):
             mixed = []
             for k in range(MIX):
                 c = i * MIX + k
-                modes = [pool[tri[q, c]].astype(F32) for q in range(PAIRS)]
+                modes = []
+                for q in range(PAIRS):
+                    block = pool[lax.div(tri[q, c], 2)].astype(F32)
+                    wanted = side == lax.rem(tri[q, c], 2)
+                    modes.append(jnp.where(wanted, block, 0.0))
                 modes = (modes[0] + modes[1]) + (modes[2] + modes[3])
-                modes = jnp.concatenate([modes[:, :TRIP], modes[:, TRIP:]], axis=0)
-                mixed.append((jnp.concatenate([modes] * 4, axis=1) * keep).astype(BF16))
+                modes = modes + pltpu.roll(modes, TRIP, 1)
+                modes = jnp.concatenate([modes, modes], axis=1) * keep
+                modes = jnp.concatenate([modes, jnp.zeros((HPAD - HARM, 4 * TRIP), F32)], axis=0)
+                mixed.append(modes.astype(BF16))
             spectrum[pl.ds(i * MIX, MIX)] = jnp.stack(mixed)
 
         loop(NBLOCK // MIX, mix)
@@ -296,16 +310,16 @@
         )
 
         def talk(j):
-            g = (s + 1 + j) % N_SRC
+            g = (s + 3 + 3 * j) % N_SRC
             parts = [
                 dot(cols[g * BPC + i].astype(BF16), lifted[g * BPC + i]) for i in range(BPC)
             ]
             pre = base[span(g), :] + jnp.concatenate(parts, axis=0)
-            put_rows(msg, g, (silu(pre) * live_of(g)).astype(BF16))
+            put_rows(msg, g, (silu_of_half(pre) * live_of(g)).astype(BF16))
 
             def send(i):
                 for k in range(4):
-                    t = (d + 1 + i * 4 + k) % N_DST
+                    t = lax.rem(d + 1 + i * 4 + k, N_DST)
                     b = g * N_DST + t
 
                     @pl.when(b != me)
@@ -317,7 +331,7 @@
         loop(N_SRC, talk)
 
         def listen(j):
-            g = (s + N_SRC - 1 - j) % N_SRC
+            g = (s + 4 * N_SRC - 3 - 3 * j) % N_SRC
 
             @pl.when(g != s)
             def _():
@@ -336,7 +350,7 @@
                 axis=0,
             )
             symmetric = (rows_of(msg, g).astype(F32) + mirrored).astype(BF16)
-            inner = silu(dot(symmetric, edge[level, 1])).astype(BF16)
+            inner = silu_of_half(dot(symmetric, edge[level, 1])).astype(BF16)
             value = (symmetric.astype(F32) + dot(inner, edge[level, 2])).astype(BF16)
             put_rows(refined, g, value)
             sums = total[...]
@@ -379,6 +393,7 @@
         for i in range(1, N_SRC):
             sums += gathered[i].astype(F32)
         sums = (sums * DEGREE ** (-0.5)).astype(BF16)
+        sums = dot(sums, edge[level, 3]).astype(BF16)
         atoms[...] = sums
         near = home // 2
         slot = home % 2
@@ -401,15 +416,12 @@
             drain(arr.at[pl.ds(0, 2 * N_DST)], atom_recv)
             drain(arr.at[pl.ds(0, 2 * N_DST)], atom_send)
 
-        known = dot(region[...].reshape(2 * ATOM_ROWS, WIDTH), edge[level, 3]).astype(BF16)
-        region[...] = known.reshape(region.shape)
-
         def update(g):
             chosen = pick[pl.ds(g * WIDE * BPC, WIDE * BPC)]
             chosen = chosen.reshape(WIDE * CHUNK, 2 * ATOM_ROWS)
             feed = dot(chosen, region[...].reshape(2 * ATOM_ROWS, WIDTH))
-            first = silu(base[span(g, WIDE), :] + feed).astype(BF16)
-            second = silu(dot(first, edge[level, 4])).astype(BF16)
+            first = silu_of_half(base[span(g, WIDE), :] + feed).astype(BF16)
+            second = silu_of_half(dot(first, edge[level, 4])).astype(BF16)
             fresh = (
                 rows_of(state, g, WIDE).astype(F32)
                 + rows_of(refined, g, WIDE).astype(F32)
@@ -421,12 +433,7 @@
             @pl.when(level < NBLK - 1)
             def _():
                 lower(level + 1, g, fresh)
-                share(g * WIDE * BPC, WIDE * BPC)
-
-            @pl.when(level == NBLK - 1)
-            def _():
-                piece = pl.ds(g * WIDE * N_DST, WIDE * N_DST)
-                pltpu.make_async_copy(state.at[piece], out.at[piece], out_sem).start()
+                share(g * WIDE, WIDE)
 
         loop(N_SRC // WIDE, update)
 
@@ -435,7 +442,6 @@
             loop(N_SRC, lambda g: base_of(level + 1, g))
 
     loop(NBLK, run_level)
-    drain(state, out_sem)
 
 
 def body(
@@ -448,11 +454,10 @@
     edges = pltpu.VMEM((DEVS, CAP, WIDTH), BF16)
     out = pl.pallas_call(
         kernel,
-        out_shape=jax.ShapeDtypeStruct((DEVS, CAP, WIDTH), BF16),
+        out_shape=pltpu.VMEM((DEVS, CAP, WIDTH), BF16),
         in_specs=[pl.BlockSpec(memory_space=pltpu.SMEM)] + [vmem] * 5 + [hbm] * 4,
-        out_specs=hbm,
+        out_specs=vmem,
         scratch_shapes=[
-            edges,
             pltpu.VMEM((ROWS, WIDTH), F32),
             edges,
             edges,
@@ -461,7 +466,7 @@
             pltpu.VMEM((NBLOCK, HPAD, BLK), F32),
             pltpu.VMEM((NBLOCK, HPAD, BLK), BF16),
             pltpu.VMEM((NBLOCK, BLK, HPAD), F32),
-            pltpu.VMEM((N_SRC * NBLOCK, HPAD // 2, 2 * TRIP), BF16),
+            pltpu.VMEM((N_SRC * N_SRC, HARM, 2 * TRIP), BF16),
             pltpu.VMEM((NBLOCK, HPAD, 4 * TRIP), BF16),
             pltpu.VMEM((NBLOCK, HPAD, WIDTH), BF16),
             pltpu.VMEM((NBLOCK, ATOM_ROWS, BLK), BF16),
@@ -476,7 +481,6 @@
             pltpu.VMEM((PIECE, WIDTH), BF16),
             pltpu.VMEM((2, N_SRC, PIECE, WIDTH), BF16),
             dma((4,)),
-            dma,
             dma,
             dma((N_SRC,)),
             dma,

time: 134 us -> 125 us (0.933)
  Pallas kernels: 131 us -> 123 us
  local copies, waits for them, and re-layouts: 3.05 us -> 1.32 us
    pallas_call x1, Pallas kernels: 131 us -> 123 us  [body(): pl.pallas_call(kernel, out_shape=pltpu.VMEM((DEVS, CAP, WIDTH), BF16), in...]
    unnamed x1, local copies, waits for them, and re-layouts: 3.05 us -> 1.32 us
where the time goes in v3:
time: 125 us
  Pallas kernels  123 us (98%)
  local copies, waits for them, and re-layouts  1.32 us (1%)
    pallas_call x1, Pallas kernels, body(): pl.pallas_call(kernel, out_shape=pltpu.VMEM((DEVS, CAP, WIDTH), BF16), in...  123 us

profile of v3, /device:TPU:1, one launch (start us, length us, event | category | flops | bytes accessed | tf_op | source)
XLA Modules:
  0.0 124.6 jit_solution(16595124336497803933)
XLA Ops:
  0.0 123.2 %shard_map.100 = bf16[128,16,512]{2,1,0:T(8,128)(2,1)S(1)} custom-call(s32[4,16]{1,0:T(4,128)} %bitcast.13, f32[3,2048]{1,0:T(4,128)} %dirs_in.1, s32[16,128]{1,0:T(8,128)} %bitcast.10, s32[16,128]{1,0:T(8,128)} %bitcast.11, s32[16,128]{1,0:T(8,128)} %bitcast.12, s32[1,128]{1,0:T(1,128)} %counts_in.1, bf16[128,16,512]{2,1,0:T(8,128)(2,1)} %bitcast.8, ...), custom_call_target="tpu_custom_call" | custom-call | tf_op jit(solution)/shard_map/pallas_call | solution.py:455
  123.3 1.3 %copy.12 = bf16[2048,512]{1,0:T(8,128)(2,1)} copy(bf16[2048,512]{1,0:T(8,128)(2,1)S(1)} %bitcast.7) | data formatting | bytes 4194304

commit v4 on v3

--- a/solution.py
+++ b/solution.py
@@ -22,9 +22,10 @@
 NBLOCK = ROWS // BLK
 BPC = CHUNK // BLK
 MIX = 4
-WIDE = 2
+WIDE = 4
 ATOM_ROWS = 256
-PIECE = ATOM_ROWS // N_SRC
+HALVES = 2
+PIECE = ATOM_ROWS // N_SRC // HALVES
 FAR = sorted(
     ((i, j) for i in range(4) for j in range(4)),
     key=lambda p: -min(p[0], 4 - p[0]) - min(p[1], 4 - p[1]),
@@ -244,7 +245,7 @@
     loads[0].wait()
     loads[1].wait()
     down[...] = down[...] * 0.5
-    loop(N_SRC, lambda g: lower(0, g, rows_of(state, g)))
+    loop(N_SRC // WIDE, lambda g: lower(0, g, rows_of(state, g, WIDE)))
     pl.semaphore_wait(barrier, DEVS - 1)
     share(0, N_SRC)
 
@@ -319,7 +320,7 @@
 
             def send(i):
                 for k in range(4):
-                    t = lax.rem(d + 1 + i * 4 + k, N_DST)
+                    t = lax.rem(z + k + 2, 4) * 4 + lax.rem(y + i + 2, 4)
                     b = g * N_DST + t
 
                     @pl.when(b != me)
@@ -359,16 +360,22 @@
             total[...] = sums
 
         loop(N_SRC, listen)
-        part[...] = total[...].astype(BF16).reshape(N_SRC, PIECE, WIDTH)
-        for hop in range(N_SRC):
-            t = (s + hop) % N_SRC
-            td = ((z + t // 2 + 2 * (t % 2)) % 4) * 4 + y
-
-            @pl.when((t != s) | (td != d))
-            def _():
-                remote(
-                    part.at[t], gathered.at[s], part_send, part_recv, t, td
-                ).start()
+        part[...] = total[...].astype(BF16).reshape(part.shape)
+        for half in range(HALVES):
+            for hop in (4, 3, 5, 2, 6, 1, 7, 0):
+                t = (s + hop) % N_SRC
+                td = ((z + t // 2 + 2 * (t % 2)) % 4) * 4 + y
+
+                @pl.when((t != s) | (td != d))
+                def _():
+                    remote(
+                        part.at[half, t],
+                        gathered.at[half, s],
+                        part_send,
+                        part_recv.at[half],
+                        t,
+                        td,
+                    ).start()
 
         def ahead(g):
             base[span(g), :] = dot(rows_of(refined, g), edge[level, 3])
@@ -378,36 +385,55 @@
         total[...] = jnp.zeros_like(total)
         drain(arr.at[pl.ds(0, DEVS - 1)], msg_send)
 
+        near = home // 2
+        slot = home % 2
+        for half in range(HALVES):
+
+            @pl.when(home == d)
+            def _():
+                gathered[half, pl.ds(s, 1)] = part[half, pl.ds(s, 1)]
+                drain(gathered.at[half, pl.ds(0, N_SRC - 1)], part_recv.at[half])
+
+            @pl.when(home != d)
+            def _():
+                drain(gathered.at[half], part_recv.at[half])
+
+            sums = gathered[half, 0].astype(F32)
+            for i in range(1, N_SRC):
+                sums += gathered[half, i].astype(F32)
+            sums = (sums * DEGREE ** (-0.5)).astype(BF16)
+            sums = dot(sums, edge[level, 3]).astype(BF16)
+            atoms[half] = sums
+
+            @pl.when(near == s)
+            def _():
+                region[pl.ds(slot, 1), half, pl.ds(s, 1)] = sums[None, None]
+
+            for far in FAR:
+                t = ((z + far[0]) % 4) * 4 + (y + far[1]) % 4
+
+                @pl.when(near * N_DST + t != me)
+                def _():
+                    remote(
+                        atoms.at[half],
+                        region.at[slot, half, s],
+                        atom_send,
+                        atom_recv,
+                        near,
+                        t,
+                    ).start()
+
         @pl.when(home == d)
         def _():
-            gathered[pl.ds(s, 1)] = part[pl.ds(s, 1)]
-            drain(gathered.at[pl.ds(0, N_SRC - 1)], part_recv)
-            drain(gathered.at[pl.ds(0, N_SRC - 1)], part_send)
+            drain(gathered.at[0], part_send)
+            drain(gathered.at[1, pl.ds(0, N_SRC - 2)], part_send)
 
         @pl.when(home != d)
         def _():
-            drain(gathered, part_recv)
             drain(gathered, part_send)
-
-        sums = gathered[0].astype(F32)
-        for i in range(1, N_SRC):
-            sums += gathered[i].astype(F32)
-        sums = (sums * DEGREE ** (-0.5)).astype(BF16)
-        sums = dot(sums, edge[level, 3]).astype(BF16)
-        atoms[...] = sums
-        near = home // 2
-        slot = home % 2
-
-        for far in FAR:
-            t = ((z + far[0]) % 4) * 4 + (y + far[1]) % 4
-
-            @pl.when(near * N_DST + t != me)
-            def _():
-                remote(atoms, region.at[slot, s], atom_send, atom_recv, near, t).start()
 
         @pl.when(near == s)
         def _():
-            region[pl.ds(slot, 1), pl.ds(s, 1)] = sums[None, None]
             drain(arr.at[pl.ds(0, 2 * (N_DST - 1))], atom_recv)
             drain(arr.at[pl.ds(0, 2 * (N_DST - 1))], atom_send)
 
@@ -476,17 +502,17 @@
             pltpu.VMEM(trip_w.shape, BF16),
             pltpu.VMEM(edge_w.shape, BF16),
             pltpu.VMEM((ATOM_ROWS, WIDTH), F32),
-            pltpu.VMEM((N_SRC, PIECE, WIDTH), BF16),
-            pltpu.VMEM((N_SRC, PIECE, WIDTH), BF16),
-            pltpu.VMEM((PIECE, WIDTH), BF16),
-            pltpu.VMEM((2, N_SRC, PIECE, WIDTH), BF16),
+            pltpu.VMEM((HALVES, N_SRC, PIECE, WIDTH), BF16),
+            pltpu.VMEM((HALVES, N_SRC, PIECE, WIDTH), BF16),
+            pltpu.VMEM((HALVES, PIECE, WIDTH), BF16),
+            pltpu.VMEM((2, HALVES, N_SRC, PIECE, WIDTH), BF16),
             dma((4,)),
             dma,
             dma((N_SRC,)),
             dma,
             dma((N_SRC,)),
             dma,
-            dma,
+            dma((HALVES,)),
             dma,
             dma,
         ],

time: 125 us -> 123 us (0.984)
  Pallas kernels: 123 us -> 121 us
    pallas_call x1, Pallas kernels: 123 us -> 121 us  [body(): pl.pallas_call(kernel, out_shape=pltpu.VMEM((DEVS, CAP, WIDTH), BF16), in...]
where the time goes in v4:
time: 123 us
  Pallas kernels  121 us (98%)
  local copies, waits for them, and re-layouts  1.32 us (1%)
    pallas_call x1, Pallas kernels, body(): pl.pallas_call(kernel, out_shape=pltpu.VMEM((DEVS, CAP, WIDTH), BF16), in...  121 us

profile of v4, /device:TPU:1, one launch (start us, length us, event | category | flops | bytes accessed | tf_op | source)
XLA Modules:
  0.0 122.5 jit_solution(11293226556769787681)
XLA Ops:
  0.0 121.2 %shard_map.100 = bf16[128,16,512]{2,1,0:T(8,128)(2,1)S(1)} custom-call(s32[4,16]{1,0:T(4,128)} %bitcast.13, f32[3,2048]{1,0:T(4,128)} %dirs_in.1, s32[16,128]{1,0:T(8,128)} %bitcast.10, s32[16,128]{1,0:T(8,128)} %bitcast.11, s32[16,128]{1,0:T(8,128)} %bitcast.12, s32[1,128]{1,0:T(1,128)} %counts_in.1, bf16[128,16,512]{2,1,0:T(8,128)(2,1)} %bitcast.8, ...), custom_call_target="tpu_custom_call" | custom-call | tf_op jit(solution)/shard_map/pallas_call | solution.py:481
  121.2 1.3 %copy.12 = bf16[2048,512]{1,0:T(8,128)(2,1)} copy(bf16[2048,512]{1,0:T(8,128)(2,1)S(1)} %bitcast.7) | data formatting | bytes 4194304

commit v5 on v4

--- a/solution.py
+++ b/solution.py
@@ -162,14 +162,13 @@
     def signal(ts, td):
         pl.semaphore_signal(barrier, inc=1, device_id=(ts, td), device_id_type=MESH)
 
-    lines = [(s + hop) % N_SRC for hop in range(N_SRC)]
-
-    def greet(i):
-        td = (d + 1 + i) % N_DST
+    lines = [lax.rem(s + hop, N_SRC) for hop in range(N_SRC)]
+    stacks = [lax.rem(z + hop, 4) * 4 for hop in range(4)]
+    rows = [lax.rem(y + hop, 4) for hop in range(4)]
+
+    for far in FAR[:-1]:
         for ts in lines:
-            signal(ts, td)
-
-    loop(N_DST - 1, greet)
+            signal(ts, stacks[far[0]] + rows[far[1]])
     for ts in lines[1:]:
         signal(ts, d)
     total[...] = jnp.zeros_like(total)
@@ -194,15 +193,14 @@
     planes = harmonics(split[:, 0, :], split[:, 1, :], split[:, 2, :])
     for i, plane in enumerate(planes):
         field[:, i, :] = plane
-    rows_y[...] = field[...].astype(BF16)
-    field[:, HARM, :] = (slot.astype(F32) < filled).astype(F32)
+    live = (slot.astype(F32) < filled).astype(F32)
+    rows_y[...] = (field[...] * live[:, None, :]).astype(BF16)
+    field[:, HARM, :] = live
     field[:, HARM + 1, :] = src_in[...].astype(F32)
     field[:, HARM + 2, :] = (lane - slot + rev_in[...]).astype(F32)
 
     def turn(c):
         cols[c] = field[c].T
-
-    loop(NBLOCK, turn)
 
     def rows_of(ref, g, n=1):
         return ref[pl.ds(g * n * N_DST, n * N_DST)].reshape(n * CHUNK, WIDTH)
@@ -219,7 +217,7 @@
         low = lax.dot_general(
             value, down[level], (((1,), (1,)), ((), ())), preferred_element_type=F32
         )
-        low = (silu_of_half(low) * live_of(g, n)).astype(BF16)
+        low = silu_of_half(low).astype(BF16)
         modes = []
         for i in range(n * BPC):
             c = g * n * BPC + i
@@ -249,18 +247,26 @@
     pl.semaphore_wait(barrier, DEVS - 1)
     share(0, N_SRC)
 
+    place = iota((BLK, 2 * ATOM_ROWS), 1)
+    group = ATOM_ROWS // HALVES
+    half_of = place // (2 * group)
+    slot_of = place // group - 2 * half_of
+    atom_of = (slot_of * ATOM_ROWS + half_of * group + place % group).astype(F32)
+
     def choose(c):
         column = cols[c]
         source = column[:, HARM + 1 : HARM + 2]
         target = column[:, HARM + 2 : HARM + 3]
         alive = column[:, HARM : HARM + 1]
-        pick[c] = (source == iota((BLK, 2 * ATOM_ROWS), 1).astype(F32)).astype(F32).astype(BF16)
+        pick[c] = (source == atom_of).astype(F32).astype(BF16)
         same = (target == iota((BLK, BLK), 1).astype(F32)).astype(F32)
         mirror[c] = (same * alive).astype(BF16)
-        onehot[c] = (
+        half = pl.ds(pl.multiple_of(lax.rem(c, BPC) * BLK, BLK), BLK)
+        onehot[lax.div(c, BPC), :, half] = (
             (iota((ATOM_ROWS, BLK), 0) == dst_in[pl.ds(c, 1), :]).astype(F32).astype(BF16)
         )
 
+    loop(NBLOCK, turn)
     loop(NBLOCK, choose)
 
     def halve(level):
@@ -319,8 +325,9 @@
             put_rows(msg, g, (silu_of_half(pre) * live_of(g)).astype(BF16))
 
             def send(i):
+                row = lax.rem(y + i + 2, 4)
                 for k in range(4):
-                    t = lax.rem(z + k + 2, 4) * 4 + lax.rem(y + i + 2, 4)
+                    t = stacks[(k + 2) % 4] + row
                     b = g * N_DST + t
 
                     @pl.when(b != me)
@@ -331,40 +338,39 @@
 
         loop(N_SRC, talk)
 
+        def arrived(g):
+            @pl.when(g != s)
+            def _():
+                drain(arr.at[pl.ds(g * N_DST, N_DST)], msg_recv.at[g])
+
+            @pl.when(g == s)
+            def _():
+                drain(arr.at[pl.ds(0, N_DST - 1)], msg_recv.at[g])
+
         def listen(j):
-            g = (s + 4 * N_SRC - 3 - 3 * j) % N_SRC
-
-            @pl.when(g != s)
-            def _():
-                drain(arr.at[pl.ds(g * N_DST, N_DST)], msg_recv.at[g])
-
-            @pl.when(g == s)
-            def _():
-                drain(arr.at[pl.ds(0, N_DST - 1)], msg_recv.at[g])
-
-            came = rows_of(arr, g)
-            mirrored = jnp.concatenate(
-                [
-                    dot(mirror[g * BPC + i], came[i * BLK : (i + 1) * BLK])
-                    for i in range(BPC)
-                ],
-                axis=0,
-            )
-            symmetric = (rows_of(msg, g).astype(F32) + mirrored).astype(BF16)
+            chunks = [(s + 4 * N_SRC - 3 - 3 * (2 * j + k)) % N_SRC for k in range(2)]
+            for g in chunks:
+                arrived(g)
+            mirrored = []
+            for g in chunks:
+                came = rows_of(arr, g)
+                for i in range(BPC):
+                    mirrored.append(dot(mirror[g * BPC + i], came[i * BLK : (i + 1) * BLK]))
+            own = jnp.concatenate([rows_of(msg, g) for g in chunks], axis=0)
+            symmetric = (own.astype(F32) + jnp.concatenate(mirrored, axis=0)).astype(BF16)
             inner = silu_of_half(dot(symmetric, edge[level, 1])).astype(BF16)
             value = (symmetric.astype(F32) + dot(inner, edge[level, 2])).astype(BF16)
-            put_rows(refined, g, value)
-            sums = total[...]
-            for i in range(BPC):
-                sums += dot(onehot[g * BPC + i], value[i * BLK : (i + 1) * BLK])
-            total[...] = sums
-
-        loop(N_SRC, listen)
+            hits = jnp.concatenate([onehot[g] for g in chunks], axis=1)
+            total[...] += dot(hits, value)
+            for k in range(2):
+                put_rows(refined, chunks[k], value[k * CHUNK : (k + 1) * CHUNK])
+
+        loop(N_SRC // 2, listen)
         part[...] = total[...].astype(BF16).reshape(part.shape)
         for half in range(HALVES):
             for hop in (4, 3, 5, 2, 6, 1, 7, 0):
-                t = (s + hop) % N_SRC
-                td = ((z + t // 2 + 2 * (t % 2)) % 4) * 4 + y
+                t = lines[hop]
+                td = lax.rem(z + lax.div(t, 2) + 2 * lax.rem(t, 2), 4) * 4 + y
 
                 @pl.when((t != s) | (td != d))
                 def _():
@@ -407,18 +413,18 @@
 
             @pl.when(near == s)
             def _():
-                region[pl.ds(slot, 1), half, pl.ds(s, 1)] = sums[None, None]
+                region[half, pl.ds(slot, 1), pl.ds(s, 1)] = sums[None, None]
 
             for far in FAR:
-                t = ((z + far[0]) % 4) * 4 + (y + far[1]) % 4
+                t = stacks[far[0]] + rows[far[1]]
 
                 @pl.when(near * N_DST + t != me)
                 def _():
                     remote(
                         atoms.at[half],
-                        region.at[slot, half, s],
-                        atom_send,
-                        atom_recv,
+                        region.at[half, slot, s],
+                        atom_send.at[half],
+                        atom_recv.at[half],
                         near,
                         t,
                     ).start()
@@ -432,21 +438,33 @@
         def _():
             drain(gathered, part_send)
 
-        @pl.when(near == s)
-        def _():
-            drain(arr.at[pl.ds(0, 2 * (N_DST - 1))], atom_recv)
-            drain(arr.at[pl.ds(0, 2 * (N_DST - 1))], atom_send)
-
-        @pl.when(near != s)
-        def _():
-            drain(arr.at[pl.ds(0, 2 * N_DST)], atom_recv)
-            drain(arr.at[pl.ds(0, 2 * N_DST)], atom_send)
+        def feed_of(half, g):
+            columns = pick[pl.ds(g * WIDE * BPC, WIDE * BPC), :, half * ATOM_ROWS : (half + 1) * ATOM_ROWS]
+            return dot(
+                columns.reshape(WIDE * CHUNK, ATOM_ROWS),
+                region[half].reshape(ATOM_ROWS, WIDTH),
+            )
+
+        def await_half(half):
+            @pl.when(near == s)
+            def _():
+                drain(arr.at[pl.ds(0, N_DST - 1)], atom_recv.at[half])
+                drain(arr.at[pl.ds(0, N_DST - 1)], atom_send.at[half])
+
+            @pl.when(near != s)
+            def _():
+                drain(arr.at[pl.ds(0, N_DST)], atom_recv.at[half])
+                drain(arr.at[pl.ds(0, N_DST)], atom_send.at[half])
+
+        def early(g):
+            base[span(g, WIDE), :] += feed_of(0, g)
+
+        await_half(0)
+        loop(N_SRC // WIDE, early)
+        await_half(1)
 
         def update(g):
-            chosen = pick[pl.ds(g * WIDE * BPC, WIDE * BPC)]
-            chosen = chosen.reshape(WIDE * CHUNK, 2 * ATOM_ROWS)
-            feed = dot(chosen, region[...].reshape(2 * ATOM_ROWS, WIDTH))
-            first = silu_of_half(base[span(g, WIDE), :] + feed).astype(BF16)
+            first = silu_of_half(base[span(g, WIDE), :] + feed_of(1, g)).astype(BF16)
             second = silu_of_half(dot(first, edge[level, 4])).astype(BF16)
             fresh = (
                 rows_of(state, g, WIDE).astype(F32)
@@ -458,8 +476,9 @@
 
             @pl.when(level < NBLK - 1)
             def _():
-                lower(level + 1, g, fresh)
-                share(g * WIDE, WIDE)
+                for k in range(2):
+                    lower(level + 1, 2 * g + k, rows_of(state, 2 * g + k, WIDE // 2))
+                    share(g * WIDE + k * WIDE // 2, WIDE // 2)
 
         loop(N_SRC // WIDE, update)
 
@@ -495,7 +514,7 @@
             pltpu.VMEM((N_SRC * N_SRC, HARM, 2 * TRIP), BF16),
             pltpu.VMEM((NBLOCK, HPAD, 4 * TRIP), BF16),
             pltpu.VMEM((NBLOCK, HPAD, WIDTH), BF16),
-            pltpu.VMEM((NBLOCK, ATOM_ROWS, BLK), BF16),
+            pltpu.VMEM((N_SRC, ATOM_ROWS, CHUNK), BF16),
             pltpu.VMEM((NBLOCK, BLK, BLK), BF16),
             pltpu.VMEM((NBLOCK, BLK, 2 * ATOM_ROWS), BF16),
             pltpu.VMEM(down.shape, BF16),
@@ -505,7 +524,7 @@
             pltpu.VMEM((HALVES, N_SRC, PIECE, WIDTH), BF16),
             pltpu.VMEM((HALVES, N_SRC, PIECE, WIDTH), BF16),
             pltpu.VMEM((HALVES, PIECE, WIDTH), BF16),
-            pltpu.VMEM((2, HALVES, N_SRC, PIECE, WIDTH), BF16),
+            pltpu.VMEM((HALVES, 2, N_SRC, PIECE, WIDTH), BF16),
             dma((4,)),
             dma,
             dma((N_SRC,)),
@@ -513,8 +532,8 @@
             dma((N_SRC,)),
             dma,
             dma((HALVES,)),
-            dma,
-            dma,
+            dma((HALVES,)),
+            dma((HALVES,)),
         ],
         compiler_params=pltpu.CompilerParams(
             collective_id=0, has_side_effects=True, vmem_limit_bytes=60 << 20

time: 123 us -> 121 us (0.984)
  Pallas kernels: 121 us -> 119 us
    pallas_call x1, Pallas kernels: 121 us -> 119 us  [body(): pl.pallas_call(kernel, out_shape=pltpu.VMEM((DEVS, CAP, WIDTH), BF16), in...]
where the time goes in v5:
time: 121 us; the launch traced here: 120 us
  Pallas kernels  119 us (98%)
  local copies, waits for them, and re-layouts  1.32 us (1%)
    pallas_call x1, Pallas kernels, body(): pl.pallas_call(kernel, out_shape=pltpu.VMEM((DEVS, CAP, WIDTH), BF16), in...  119 us

profile of v5, /device:TPU:1, one launch (start us, length us, event | category | flops | bytes accessed | tf_op | source)
XLA Modules:
  0.0 120.5 jit_solution(12130579130094004909)
XLA Ops:
  0.0 119.1 %shard_map.100 = bf16[128,16,512]{2,1,0:T(8,128)(2,1)S(1)} custom-call(s32[4,16]{1,0:T(4,128)} %bitcast.13, f32[3,2048]{1,0:T(4,128)} %dirs_in.1, s32[16,128]{1,0:T(8,128)} %bitcast.10, s32[16,128]{1,0:T(8,128)} %bitcast.11, s32[16,128]{1,0:T(8,128)} %bitcast.12, s32[1,128]{1,0:T(1,128)} %counts_in.1, bf16[128,16,512]{2,1,0:T(8,128)(2,1)} %bitcast.8, ...), custom_call_target="tpu_custom_call" | custom-call | tf_op jit(solution)/shard_map/pallas_call | solution.py:500
  119.2 1.3 %copy.12 = bf16[2048,512]{1,0:T(8,128)(2,1)} copy(bf16[2048,512]{1,0:T(8,128)(2,1)S(1)} %bitcast.7) | data formatting | bytes 4194304

commit v6 on v5

--- a/solution.py
+++ b/solution.py
@@ -21,7 +21,7 @@
 CHUNK = N_DST * CAP
 NBLOCK = ROWS // BLK
 BPC = CHUNK // BLK
-MIX = 4
+MIX = 16
 WIDE = 4
 ATOM_ROWS = 256
 HALVES = 2

time: 121 us -> 120 us (level)
  no operation moved by 1% of the time
where the time goes in v6:
time: 120 us
  Pallas kernels  118 us (98%)
  local copies, waits for them, and re-layouts  1.32 us (1%)
    pallas_call x1, Pallas kernels, body(): pl.pallas_call(kernel, out_shape=pltpu.VMEM((DEVS, CAP, WIDTH), BF16), in...  118 us

profile of v6, /device:TPU:1, one launch (start us, length us, event | category | flops | bytes accessed | tf_op | source)
XLA Modules:
  0.0 119.6 jit_solution(3341310605089087870)
XLA Ops:
  0.0 118.3 %shard_map.100 = bf16[128,16,512]{2,1,0:T(8,128)(2,1)S(1)} custom-call(s32[4,16]{1,0:T(4,128)} %bitcast.13, f32[3,2048]{1,0:T(4,128)} %dirs_in.1, s32[16,128]{1,0:T(8,128)} %bitcast.10, s32[16,128]{1,0:T(8,128)} %bitcast.11, s32[16,128]{1,0:T(8,128)} %bitcast.12, s32[1,128]{1,0:T(1,128)} %counts_in.1, bf16[128,16,512]{2,1,0:T(8,128)(2,1)} %bitcast.8, ...), custom_call_target="tpu_custom_call" | custom-call | tf_op jit(solution)/shard_map/pallas_call | solution.py:500
  118.3 1.3 %copy.12 = bf16[2048,512]{1,0:T(8,128)(2,1)} copy(bf16[2048,512]{1,0:T(8,128)(2,1)S(1)} %bitcast.7) | data formatting | bytes 4194304
